TPU v7x, 32 devices: a whole 2x2x4 slice. The times are simulated.
32 devices in a mesh: rep: 8 (over z, core), mdl: 4 (over y, x).
Axes of the slice: x: 2, y: 2, z: 4, core: 2. Of those that a mesh axis runs over, the one named last changes fastest.
Arguments:
- deltas: bfloat16 [8, 2560, 2560], P('rep', 'mdl'), may hold values from -72 to 72
- errors: bfloat16 [8, 2560, 2560], P('rep', 'mdl'), may hold values from -3 to 3
- starts: float32 [2560, 64], replicated, may hold values from -6 to 6
- momentum: float32 [2560, 2560], P('mdl', 'rep'), may hold values from -2 to 2
Outputs:
- new_errors: bfloat16 [8, 2560, 2560], P('rep', 'mdl')
- new_momentum: float32 [2560, 2560], P('mdl', 'rep')
- outer_step: float32 [2560, 2560], P('mdl', 'rep')
All inputs are finite; a program needn't handle non-finite values.
Results may differ from a plain program's by a relative error of at most 0.001.
Values sent between devices are 32-bit elements; how exact they have to be, the bound alone decides.
A program may use at most 64 MiB of HBM per device.

v0:
```python
import jax
import jax.numpy as jnp
from jax import lax
from jax.sharding import PartitionSpec as P

highest = lax.Precision.HIGHEST


def body(deltas, errors, starts, momentum):
    replicas = lax.axis_size("rep")
    merged = deltas[0].astype(jnp.float32) + errors[0].astype(jnp.float32)
    left_part = jnp.einsum("ac,ck->ka", merged, starts, precision=highest)
    left = lax.psum(left_part, "rep") / replicas
    gram = jnp.einsum("ka,la->kl", left, left, precision=highest)
    gram = lax.psum(gram, "mdl")
    lower = jnp.linalg.cholesky(gram)
    basis = jax.scipy.linalg.solve_triangular(lower, left, lower=True)
    right_part = jnp.einsum("ac,ka->kc", merged, basis, precision=highest)
    column_shares = lax.psum_scatter(right_part, "mdl", scatter_dimension=1, tiled=True)
    column_shares = lax.psum(column_shares, "rep")
    right = lax.all_gather(column_shares, "mdl", axis=1, tiled=True) / replicas
    approx = jnp.einsum("ka,kc->ac", basis, right, precision=highest)
    new_errors = (merged - approx).astype(jnp.bfloat16)[None]
    width = momentum.shape[1]
    owned = lax.dynamic_slice_in_dim(approx, lax.axis_index("rep") * width, width, 1)
    new_momentum = 0.9 * momentum + owned
    outer_step = 0.7 * (owned + 0.9 * new_momentum)
    return (new_errors, new_momentum, outer_step)


def solution(mesh):
    placed = (P("rep", "mdl", None), P("rep", "mdl", None), P(), P("mdl", "rep"))
    return jax.shard_map(
        body,
        mesh=mesh,
        in_specs=placed,
        out_specs=(P("rep", "mdl", None), P("mdl", "rep"), P("mdl", "rep")),
        check_vma=False,
    )
```

profile of v0, /device:TPU:0, one launch (start us, length us, event | category | flops | bytes accessed | tf_op | source)
XLA Modules:
  0.0 226.7 jit_solution(16170956885530419653)
XLA Ops:
  7.2 0.0 copy-start
  7.2 0.0 copy-start.3
  7.2 0.0 all-reduce.3.cloned.1.call-start
  7.2 1.0 copy-done
  8.3 9.4 %fusion.6 = f32[64,640]{1,0:T(8,128)} fusion(f32[2560,64]{0,1:T(8,128)S(1)} %copy-done, bf16[1,640,2560]{2,1,0:T(8,128)(2,1)} %param.5, bf16[1,640,2560]{2,1,0:T(8,128)(2,1)} %param.4), kind=kOutput, calls=%fused_computation.8 | convolution fusion | flops 1263206400 | bytes 7372800 | tf_op jit(solution)/shard_map/ac,ck->ka/dot_general | solution.py:12
  17.6 0.0 all-reduce.3.cloned.1.call-update
  17.7 0.0 reduce-scatter.2.cloned.1.call-start
  17.7 55.5 %all-reduce.3.cloned.1.call-done = f32[64,640]{1,0:T(8,128)} async-done(((f32[64,640]{1,0:T(8,128)}), f32[64,640]{1,0:T(8,128)}) %all-reduce.3.cloned.1.call-update) | async-done | bytes 163856 | tf_op jit(solution)/shard_map/psum | solution.py:13
  73.2 1.3 fusion.14
  74.5 16.2 %psum.22 = f32[64,64]{0,1:T(8,128)S(1)} all-reduce(f32[64,64]{0,1:T(8,128)S(1)} %fusion.14), channel_id=1, replica_groups=mesh['rep'=8,'mdl'=4] {'mdl'}, use_global_device_ids=true, to_apply=%region_1.0 | all-reduce | flops 4096 | bytes 32768 | tf_op jit(solution)/shard_map/psum | solution.py:15
  90.7 0.1 copy.8
  90.8 5.8 %cholesky.16 = f32[64,64]{1,0:T(8,128)S(1)} custom-call(f32[64,64]{1,0:T(8,128)S(1)} %fusion.20), custom_call_target="Cholesky" | custom-call | tf_op jit(solution)/shard_map/jit(cholesky)/cholesky | solution.py:16
  96.7 0.6 compare_reduce_fusion
  97.3 0.7 fusion.18
  98.0 4.9 %custom-call.7 = f32[1,64,64]{1,2,0:T(8,128)S(1)} custom-call(f32[1,64,64]{2,1,0:T(8,128)S(1)} %fusion.18), custom_call_target="InvertDiagBlocksLowerTriangular" | custom-call | tf_op jit(solution)/shard_map/jit(_solve_triangular)/triangular_solve | solution.py:17
  102.9 1.3 fusion.12
  104.2 8.3 %fusion = f32[64,2560]{1,0:T(8,128)} fusion(f32[64,640]{1,0:T(8,128)S(1)} %fusion.12, bf16[1,640,2560]{2,1,0:T(8,128)(2,1)} %param.5, bf16[1,640,2560]{2,1,0:T(8,128)(2,1)} %param.4), kind=kOutput, calls=%fused_computation.1 | convolution fusion | flops 1263206400 | bytes 7372800 | tf_op jit(solution)/shard_map/ac,ka->kc/dot_general | solution.py:18
  112.5 0.0 reduce-scatter.2.cloned.1.call-update
  112.5 0.0 all-reduce.5.cloned.1.call-start
  112.6 25.6 %reduce-scatter.2.cloned.1.call-done = f32[64,640]{1,0:T(8,128)} async-done(((f32[64,2560]{1,0:T(8,128)}), f32[64,640]{1,0:T(8,128)}) %reduce-scatter.2.cloned.1.call-update) | async-done | bytes 163856 | tf_op jit(solution)/shard_map/reduce_scatter | solution.py:19
  138.2 0.0 all-reduce.5.cloned.1.call-update
  138.3 0.0 copy-done.3
  138.3 0.3 copy.9
  138.6 54.7 %all-reduce.5.cloned.1.call-done = f32[64,640]{1,0:T(8,128)} async-done(((f32[64,640]{1,0:T(8,128)}), f32[64,640]{1,0:T(8,128)}) %all-reduce.5.cloned.1.call-update) | async-done | bytes 163856 | tf_op jit(solution)/shard_map/psum | solution.py:20
  193.3 0.0 copy-start.1
  193.3 0.0 copy-start.2
  193.3 13.2 %all_gather.3 = f32[64,2560]{1,0:T(8,128)S(1)} all-gather(f32[64,640]{1,0:T(8,128)} %all-reduce.5.cloned.1.call-done), channel_id=1, replica_groups=mesh['rep'=8,'mdl'=4] {'mdl'}, dimensions={1}, use_global_device_ids=true | all-gather | bytes 819200 | tf_op jit(solution)/shard_map/all_gather | solution.py:21
  206.4 5.4 %fusion.9 = f32[640,2560]{1,0:T(8,128)S(1)} fusion(f32[64,640]{1,0:T(8,128)S(1)} %fusion.12, f32[64,2560]{1,0:T(8,128)S(1)} %all_gather.3), kind=kOutput, calls=%fused_computation.11 | convolution fusion | flops 1258455040 | bytes 7372800 | tf_op jit(solution)/shard_map/ka,kc->ac/dot_general | solution.py:22
  211.9 0.0 copy-done.1
  211.9 0.0 copy-done.2
  211.9 3.3 %fusion.5 = bf16[1,640,2560]{2,1,0:T(8,128)(2,1)} fusion(f32[640,2560]{1,0:T(8,128)S(1)} %fusion.9, bf16[1,640,2560]{2,1,0:T(8,128)(2,1)S(1)} %copy-done.1, bf16[1,640,2560]{2,1,0:T(8,128)(2,1)S(1)} %copy-done.2), kind=kLoop, calls=%fused_computation.7 | loop fusion | flops 8192000 | bytes 16384000 | tf_op jit(solution)/shard_map/broadcast_in_dim | solution.py:23
  215.2 1.3 add_multiply_fusion
  216.5 2.4 %copy.10 = f32[640,320]{0,1:T(8,128)} copy(f32[640,320]{1,0:T(8,128)} %get-tuple-element.7) | data formatting | bytes 1638400
  218.9 1.2 copy.11
  (2 shorter events, 0.0 us)
Async XLA Ops:
  7.2 1.1 copy-start
  7.2 131.1 %copy-start.3 = (f32[640,320]{0,1:T(8,128)S(1)}, f32[640,320]{0,1:T(8,128)}, u32[]{:S(2)}) copy-start(f32[640,320]{0,1:T(8,128)} %param.7) | copy-start | bytes 2457604
  7.2 66.0 %all-reduce.3.cloned.1.call-start = ((), (), s32[]{:S(2)}) async-start(), calls=%async_computation.1 | async-start | bytes 327680 | tf_op jit(solution)/shard_map/psum | solution.py:13
  17.7 120.6 %reduce-scatter.2.cloned.1.call-start = ((), (), s32[]{:S(2)}) async-start(), calls=%async_computation.2 | async-start | bytes 819200 | tf_op jit(solution)/shard_map/reduce_scatter | solution.py:19
  112.5 80.7 %all-reduce.5.cloned.1.call-start = ((), (), s32[]{:S(2)}) async-start(), calls=%async_computation.3 | async-start | bytes 327680 | tf_op jit(solution)/shard_map/psum | solution.py:20
  193.3 18.6 %copy-start.1 = (bf16[1,640,2560]{2,1,0:T(8,128)(2,1)S(1)}, bf16[1,640,2560]{2,1,0:T(8,128)(2,1)}, u32[]{:S(2)}) copy-start(bf16[1,640,2560]{2,1,0:T(8,128)(2,1)} %param.5) | copy-start | bytes 9830404
  193.3 18.6 %copy-start.2 = (bf16[1,640,2560]{2,1,0:T(8,128)(2,1)S(1)}, bf16[1,640,2560]{2,1,0:T(8,128)(2,1)}, u32[]{:S(2)}) copy-start(bf16[1,640,2560]{2,1,0:T(8,128)(2,1)} %param.4) | copy-start | bytes 9830404
Sparse Core Ops, SparseCore 0:
  17.8 55.3 all-reduce.2
  112.7 25.5 reduce-scatter.1
  140.6 52.6 all-reduce.4
where the time goes:
time: 227 us
  waiting for transfers between devices  136 us (60%)
  blocking collectives  29.4 us (13%)
  matrix products  25.7 us (11%)
  other arithmetic  16.7 us (7%)
  between operations  13.8 us (6%)
  local copies, waits for them, and re-layouts  5.06 us (2%)
    psum x1, waiting for transfers between devices, body(): left = lax.psum(left_part, 'rep') / replicas  55.5 us
    psum x1, waiting for transfers between devices, body(): column_shares = lax.psum(column_shares, 'rep')  54.7 us
    reduce_scatter x1, waiting for transfers between devices, body(): lax.psum_scatter(right_part, 'mdl', scatter_dimension=1, tiled=True)  25.6 us
    psum x1, blocking collectives, body(): gram = lax.psum(gram, 'mdl')  16.2 us
    all_gather x1, blocking collectives, body(): right = lax.all_gather(column_shares, 'mdl', axis=1, tiled=True) / replicas  13.2 us
    dot_general x1, matrix products, body(): left_part = jnp.einsum('ac,ck->ka', merged, starts, precision=highest)  9.37 us
    dot_general x1, matrix products, body(): right_part = jnp.einsum('ac,ka->kc', merged, basis, precision=highest)  8.35 us
    another operation x3, other arithmetic, body(): lower = jnp.linalg.cholesky(gram)  6.52 us
  transfers between devices with their start and end apart: 3, of which 3 were waited for; matrix products, arithmetic and copies ran while one was open for 0% of the time, Pallas kernels for 0%

commit v1 on v0

--- a/solution.py
+++ b/solution.py
@@ -10,7 +10,7 @@
     replicas = lax.axis_size("rep")
     merged = deltas[0].astype(jnp.float32) + errors[0].astype(jnp.float32)
     left_part = jnp.einsum("ac,ck->ka", merged, starts, precision=highest)
-    left = lax.psum(left_part, "rep") / replicas
+    left = jnp.sum(lax.all_gather(left_part, "rep"), axis=0) / replicas
     gram = jnp.einsum("ka,la->kl", left, left, precision=highest)
     gram = lax.psum(gram, "mdl")
     lower = jnp.linalg.cholesky(gram)

time: 227 us -> 195 us (0.86)
  waiting for transfers between devices: 136 us -> 104 us
    psum x1 -> x0, waiting for transfers between devices: 55.5 us -> none  [body(): left = lax.psum(left_part, 'rep') / replicas]
    all_gather x0 -> x1, waiting for transfers between devices: none -> 26.2 us  [body(): left = jnp.sum(lax.all_gather(left_part, 'rep'), axis=0) / replicas]
where the time goes in v1:
time: 195 us
  waiting for transfers between devices  104 us (53%)
  blocking collectives  29.4 us (15%)
  matrix products  23.8 us (12%)
  other arithmetic  18.1 us (9%)
  between operations  13.8 us (7%)
  local copies, waits for them, and re-layouts  5.07 us (3%)
    psum x1, waiting for transfers between devices, body(): column_shares = lax.psum(column_shares, 'rep')  54.6 us
    all_gather x1, waiting for transfers between devices, body(): left = jnp.sum(lax.all_gather(left_part, 'rep'), axis=0) / replicas  26.2 us
    reduce_scatter x1, waiting for transfers between devices, body(): lax.psum_scatter(right_part, 'mdl', scatter_dimension=1, tiled=True)  23.5 us
    psum x1, blocking collectives, body(): gram = lax.psum(gram, 'mdl')  16.2 us
    all_gather x1, blocking collectives, body(): right = lax.all_gather(column_shares, 'mdl', axis=1, tiled=True) / replicas  13.2 us
    dot_general x1, matrix products, body(): left_part = jnp.einsum('ac,ck->ka', merged, starts, precision=highest)  9.38 us
    dot_general x1, matrix products, body(): right_part = jnp.einsum('ac,ka->kc', merged, basis, precision=highest)  8.35 us
    another operation x3, other arithmetic, body(): lower = jnp.linalg.cholesky(gram)  6.52 us
  transfers between devices with their start and end apart: 3, of which 3 were waited for; matrix products, arithmetic and copies ran while one was open for 0% of the time, Pallas kernels for 0%

profile of v1, /device:TPU:0, one launch (start us, length us, event | category | flops | bytes accessed | tf_op | source)
XLA Modules:
  0.0 194.8 jit_solution(664166151225650861)
XLA Ops:
  7.2 0.0 copy-start
  7.2 0.0 all-gather.3.cloned.1.call-start
  7.2 1.0 copy-done
  8.3 9.4 %fusion.6 = f32[64,640]{1,0:T(8,128)} fusion(f32[2560,64]{0,1:T(8,128)S(1)} %copy-done, bf16[1,640,2560]{2,1,0:T(8,128)(2,1)} %param.5, bf16[1,640,2560]{2,1,0:T(8,128)(2,1)} %param.4), kind=kOutput, calls=%fused_computation.8 | convolution fusion | flops 1263206400 | bytes 7372800 | tf_op jit(solution)/shard_map/ac,ck->ka/dot_general | solution.py:12
  17.6 0.0 copy-start.3
  17.6 0.0 all-gather.3.cloned.1.call-update
  17.7 0.0 reduce-scatter.2.cloned.1.call-start
  17.7 26.2 %all-gather.3.cloned.1.call-done = f32[512,640]{1,0:T(8,128)} async-done(((f32[64,640]{1,0:T(8,128)}), f32[512,640]{1,0:T(8,128)}) %all-gather.3.cloned.1.call-update) | async-done | bytes 1310736 | tf_op jit(solution)/shard_map/all_gather | solution.py:13
  43.9 1.4 reduce_sum.9
  45.3 0.3 fusion.14
  45.7 16.2 %psum.14 = f32[64,64]{0,1:T(8,128)S(1)} all-reduce(f32[64,64]{0,1:T(8,128)S(1)} %fusion.14), channel_id=1, replica_groups=mesh['rep'=8,'mdl'=4] {'mdl'}, use_global_device_ids=true, to_apply=%region_1.0 | all-reduce | flops 4096 | bytes 32768 | tf_op jit(solution)/shard_map/psum | solution.py:15
  61.9 0.1 copy.8
  62.0 5.8 %cholesky.16 = f32[64,64]{1,0:T(8,128)S(1)} custom-call(f32[64,64]{1,0:T(8,128)S(1)} %fusion.20), custom_call_target="Cholesky" | custom-call | tf_op jit(solution)/shard_map/jit(cholesky)/cholesky | solution.py:16
  67.9 0.6 compare_reduce_fusion
  68.5 0.7 fusion.18
  69.2 4.9 %custom-call.7 = f32[1,64,64]{1,2,0:T(8,128)S(1)} custom-call(f32[1,64,64]{2,1,0:T(8,128)S(1)} %fusion.18), custom_call_target="InvertDiagBlocksLowerTriangular" | custom-call | tf_op jit(solution)/shard_map/jit(_solve_triangular)/triangular_solve | solution.py:17
  74.1 0.4 fusion.12
  74.4 8.4 %fusion = f32[64,2560]{1,0:T(8,128)} fusion(f32[64,640]{1,0:T(8,128)S(1)} %fusion.12, bf16[1,640,2560]{2,1,0:T(8,128)(2,1)} %param.5, bf16[1,640,2560]{2,1,0:T(8,128)(2,1)} %param.4), kind=kOutput, calls=%fused_computation.1 | convolution fusion | flops 1263206400 | bytes 7372800 | tf_op jit(solution)/shard_map/ac,ka->kc/dot_general | solution.py:18
  82.8 0.0 reduce-scatter.2.cloned.1.call-update
  82.8 0.0 all-reduce.2.cloned.1.call-start
  82.9 23.5 %reduce-scatter.2.cloned.1.call-done = f32[64,640]{1,0:T(8,128)} async-done(((f32[64,2560]{1,0:T(8,128)}), f32[64,640]{1,0:T(8,128)}) %reduce-scatter.2.cloned.1.call-update) | async-done | bytes 163856 | tf_op jit(solution)/shard_map/reduce_scatter | solution.py:19
  106.4 0.0 all-reduce.2.cloned.1.call-update
  106.4 0.0 copy-done.3
  106.4 0.3 copy.9
  106.8 54.6 %all-reduce.2.cloned.1.call-done = f32[64,640]{1,0:T(8,128)} async-done(((f32[64,640]{1,0:T(8,128)}), f32[64,640]{1,0:T(8,128)}) %all-reduce.2.cloned.1.call-update) | async-done | bytes 163856 | tf_op jit(solution)/shard_map/psum | solution.py:20
  161.4 0.0 copy-start.1
  161.4 0.0 copy-start.2
  161.4 13.2 %all_gather.11 = f32[64,2560]{1,0:T(8,128)S(1)} all-gather(f32[64,640]{1,0:T(8,128)} %all-reduce.2.cloned.1.call-done), channel_id=1, replica_groups=mesh['rep'=8,'mdl'=4] {'mdl'}, dimensions={1}, use_global_device_ids=true | all-gather | bytes 819200 | tf_op jit(solution)/shard_map/all_gather | solution.py:21
  174.6 5.4 %fusion.9 = f32[640,2560]{1,0:T(8,128)S(1)} fusion(f32[64,640]{1,0:T(8,128)S(1)} %fusion.12, f32[64,2560]{1,0:T(8,128)S(1)} %all_gather.11), kind=kOutput, calls=%fused_computation.11 | convolution fusion | flops 1258455040 | bytes 7372800 | tf_op jit(solution)/shard_map/ka,kc->ac/dot_general | solution.py:22
  180.0 0.0 copy-done.1
  180.0 0.0 copy-done.2
  180.0 3.3 %fusion.5 = bf16[1,640,2560]{2,1,0:T(8,128)(2,1)} fusion(f32[640,2560]{1,0:T(8,128)S(1)} %fusion.9, bf16[1,640,2560]{2,1,0:T(8,128)(2,1)S(1)} %copy-done.1, bf16[1,640,2560]{2,1,0:T(8,128)(2,1)S(1)} %copy-done.2), kind=kLoop, calls=%fused_computation.7 | loop fusion | flops 8192000 | bytes 16384000 | tf_op jit(solution)/shard_map/broadcast_in_dim | solution.py:23
  183.4 1.3 add_multiply_fusion
  184.7 2.4 %copy.10 = f32[640,320]{0,1:T(8,128)} copy(f32[640,320]{1,0:T(8,128)} %get-tuple-element.7) | data formatting | bytes 1638400
  187.1 1.2 copy.11
  (2 shorter events, 0.0 us)
Async XLA Ops:
  7.2 1.1 copy-start
  7.2 36.8 %all-gather.3.cloned.1.call-start = ((), (), s32[]{:S(2)}) async-start(), calls=%async_computation.3 | async-start | bytes 1474560 | tf_op jit(solution)/shard_map/all_gather | solution.py:13
  17.6 88.8 %copy-start.3 = (f32[640,320]{0,1:T(8,128)S(1)}, f32[640,320]{0,1:T(8,128)}, u32[]{:S(2)}) copy-start(f32[640,320]{0,1:T(8,128)} %param.7) | copy-start | bytes 2457604
  17.7 88.7 %reduce-scatter.2.cloned.1.call-start = ((), (), s32[]{:S(2)}) async-start(), calls=%async_computation.1 | async-start | bytes 819200 | tf_op jit(solution)/shard_map/reduce_scatter | solution.py:19
  82.8 78.6 %all-reduce.2.cloned.1.call-start = ((), (), s32[]{:S(2)}) async-start(), calls=%async_computation.2 | async-start | bytes 327680 | tf_op jit(solution)/shard_map/psum | solution.py:20
  161.4 18.6 %copy-start.1 = (bf16[1,640,2560]{2,1,0:T(8,128)(2,1)S(1)}, bf16[1,640,2560]{2,1,0:T(8,128)(2,1)}, u32[]{:S(2)}) copy-start(bf16[1,640,2560]{2,1,0:T(8,128)(2,1)} %param.5) | copy-start | bytes 9830404
  161.4 18.6 %copy-start.2 = (bf16[1,640,2560]{2,1,0:T(8,128)(2,1)S(1)}, bf16[1,640,2560]{2,1,0:T(8,128)(2,1)}, u32[]{:S(2)}) copy-start(bf16[1,640,2560]{2,1,0:T(8,128)(2,1)} %param.4) | copy-start | bytes 9830404
Sparse Core Ops, SparseCore 0:
  17.8 26.1 all-gather.2
  82.9 23.4 reduce-scatter.1
  108.7 52.6 all-reduce.1
